TPU v7x, 32 devices: a whole 2x2x4 slice. The times are simulated.
32 devices in a mesh: dom: 16 (over z, y, x), tgt: 2 (over core).
Axes of the slice: x: 2, y: 2, z: 4, core: 2. Of those that a mesh axis runs over, the one named last changes fastest.
Arguments:
- positions: float32 [3, 16384], P(None, ('dom', 'tgt')), may hold values from -3 to 3
- normals: float32 [3, 16384], P(None, ('dom', 'tgt')), may hold values from -6 to 6
- weights: float32 [16384], P(('dom', 'tgt')), may hold values from 0.001 to 0.01
- density: float32 [32, 16384], P(None, ('dom', 'tgt')), may hold values from -6 to 6
- partners: int32 [16, 8], P('dom'), may hold values from 0 to 15, as said below
- band_list: int32 [16, 8, 8], P('dom'), may hold values from 0 to 7
- near_list: int32 [128, 24], P(('dom', 'tgt')), may hold values from 0 to 71
- near_count: int32 [128], P(('dom', 'tgt')), may hold values from 1 to 24, as said below
- singular: int32 [128, 24], P(('dom', 'tgt')), may hold values 0 or 1
Outputs:
- near_field: float32 [32, 16384], P(None, ('dom', 'tgt'))
Inputs may be any that keep to these rules, and one draw needn't show every extreme that they name: In each matching the partners pair the partitions (the partner of a partner is the partition itself, never itself), and the 8 partners of a partition are distinct. `near_count`: 24 is reached by some target tile in every draw.
All inputs are finite; a program needn't handle non-finite values. No bound on the sum of `singular` on one device may be relied on, other than what follows from the above.
Results may differ from a plain program's by a relative error of at most 0.0041.
Values sent between devices are 32-bit elements; how exact they have to be, the bound alone decides.
A program may use at most 64 MiB of HBM per device.

v0:
```python
import math
import jax
import jax.numpy as jnp
from jax import lax
from jax.sharding import PartitionSpec as P

TILE = 128
wave_number = 6.0
coupling = 1.5
narrow_core = 0.1
wide_core = 0.4


def build_kernel(target_pos, source, valid_mask, flag_row):
    offset = source[:, 0:3, :, None] - target_pos[:, :, None, :]
    core_width = jnp.where(flag_row > 0, wide_core, narrow_core)[:, None, None]
    distance = jnp.sqrt(jnp.sum(offset * offset, axis=1) + core_width * core_width)
    inverse = 1.0 / distance
    normal_part = jnp.sum(offset * source[:, 3:6, :, None], axis=1) * inverse
    radial = inverse / (4.0 * math.pi)
    cos_part = jnp.cos(wave_number * distance) * radial
    sin_part = jnp.sin(wave_number * distance) * radial
    weight_mask = source[:, 6, :, None] * valid_mask[:, None, None]
    kernel_re = weight_mask * (
        normal_part * (-cos_part * inverse - wave_number * sin_part) - coupling * sin_part
    )
    kernel_im = weight_mask * (
        normal_part * (wave_number * cos_part - sin_part * inverse) + coupling * cos_part
    )
    return jnp.concatenate([kernel_re, kernel_im], axis=1).astype(jnp.bfloat16)


def density_side(source):
    density_bf = source[:, 7:, :].astype(jnp.bfloat16)
    half_rows = density_bf.shape[1] // 2
    real_part = density_bf[:, :half_rows]
    imag_part = density_bf[:, half_rows:]
    upper = jnp.concatenate([real_part, -imag_part], axis=2)
    lower = jnp.concatenate([imag_part, real_part], axis=2)
    return jnp.concatenate([upper, lower], axis=1)


def shards(
    positions, normals, weights, density, partners, band_list, near_list, near_count, singular
):
    payload = jnp.concatenate([positions, normals, weights[None, :], density], axis=0)
    channels = payload.shape[0]
    local_tiles = payload.shape[1] // TILE
    whole_part = lax.all_gather(payload, "tgt", axis=1, tiled=True)
    part_tiles = whole_part.reshape(channels, -1, TILE).transpose(1, 0, 2)
    n_dom = lax.axis_size("dom")
    band_size = band_list.shape[2]
    my_partners = partners[0]
    send_slots = jnp.zeros((n_dom, band_size, channels, TILE), jnp.float32)
    send_slots = send_slots.at[my_partners].set(part_tiles[band_list[0]])
    arrived = lax.all_to_all(send_slots, "dom", split_axis=0, concat_axis=0, tiled=True)
    band_tiles = arrived[my_partners]
    source_pool = jnp.concatenate([part_tiles, band_tiles.reshape(-1, channels, TILE)], axis=0)
    target_pos = positions.reshape(3, local_tiles, TILE).transpose(1, 0, 2)
    pair_targets = jnp.concatenate([target_pos, target_pos], axis=0)

    def add_pair(pair_idx, totals):
        columns = lax.dynamic_slice_in_dim(near_list, 2 * pair_idx, 2, 1)
        flag_pair = lax.dynamic_slice_in_dim(singular, 2 * pair_idx, 2, 1)
        pick_idx = columns.T.reshape(-1)
        source = source_pool[pick_idx]
        entry_ids = 2 * pair_idx + jnp.arange(2, dtype=jnp.int32)
        valid_mask = (entry_ids[:, None] < near_count[None, :]).reshape(-1).astype(jnp.float32)
        kernel = build_kernel(pair_targets, source, valid_mask, flag_pair.T.reshape(-1))
        left_side = density_side(source)
        term_pairs = jnp.einsum(
            "brs,bst->brt", left_side, kernel, preferred_element_type=jnp.float32
        )
        return totals + term_pairs[:local_tiles] + term_pairs[local_tiles:]

    trip_count = (jnp.max(near_count) + 1) // 2
    start_sum = jnp.zeros((local_tiles, channels - 7, TILE), jnp.float32)
    totals = lax.fori_loop(0, trip_count, add_pair, start_sum)
    return totals.transpose(1, 0, 2).reshape(channels - 7, local_tiles * TILE)


def solution(mesh):
    in_specs = (
        P(None, ("dom", "tgt")),
        P(None, ("dom", "tgt")),
        P(("dom", "tgt")),
        P(None, ("dom", "tgt")),
        P("dom", None),
        P("dom", None, None),
        P(("dom", "tgt"), None),
        P(("dom", "tgt")),
        P(("dom", "tgt"), None),
    )
    out_specs = P(None, ("dom", "tgt"))
    return jax.shard_map(shards, mesh=mesh, in_specs=in_specs, out_specs=out_specs, check_vma=False)
```

profile of v0, /device:TPU:16, one launch (start us, length us, event | category | flops | bytes accessed | tf_op | source)
XLA Modules:
  0.0 140.2 jit_solution(14776132372673987182)
XLA Ops:
  0.0 0.9 pad_maximum_fusion.1
  0.9 1.9 %all_gather.3 = f32[39,1024]{1,0:T(8,128)S(1)} all-gather(f32[39,512]{1,0:T(8,128)S(1)} %pad_maximum_fusion.1), channel_id=1, replica_groups=mesh['dom'=16,'tgt'=2] {'tgt'}, dimensions={1}, use_global_device_ids=true | all-gather | bytes 239616 | tf_op jit(solution)/shard_map/all_gather | solution.py:49
  3.0 0.7 gather_fusion.1
  3.7 0.2 copy.29
  3.9 0.4 copy-done.5
  4.4 1.6 %broadcast_in_dim.16 = f32[16,8,39,128]{3,1,2,0:T(8,128)} broadcast(f32[]{:T(128)} %constant.16.clone.1), dimensions={} | broadcast | bytes 2555908 | tf_op jit(solution)/shard_map/broadcast_in_dim | solution.py:54
  6.0 3.1 %scatter_fusion = f32[16,8,39,128]{3,1,2,0:T(8,128)} fusion(f32[16,8,39,128]{3,1,2,0:T(8,128)} %broadcast_in_dim.16, s32[8]{0:T(128)S(1)} %fusion.19, f32[8,8,39,128]{3,1,2,0:T(8,128)S(1)} %copy.29), kind=kCustom, calls=%fused_computation.3 | custom fusion | bytes 3833888 | tf_op jit(solution)/shard_map/scatter | solution.py:55
  9.1 7.3 %all-to-all-start = ((f32[16,8,39,128]{3,1,2,0:T(8,128)}), f32[16,8,39,128]{3,1,2,0:T(8,128)S(1)}, u32[]{:S(2)}, u32[]{:S(2)}) async-start(f32[16,8,39,128]{3,1,2,0:T(8,128)} %scatter_fusion), calls=%async_computation | async-start | bytes 5111808 | tf_op jit(solution)/shard_map/all_to_all | solution.py:56
  16.4 0.6 reduce_max.9
  17.9 56.5 %all-to-all-done = f32[16,8,39,128]{3,1,2,0:T(8,128)S(1)} async-done(((f32[16,8,39,128]{3,1,2,0:T(8,128)}), f32[16,8,39,128]{3,1,2,0:T(8,128)S(1)}, u32[]{:S(2)}, u32[]{:S(2)}) %all-to-all-start) | async-done | bytes 2555936 | tf_op jit(solution)/shard_map/all_to_all | solution.py:56
  74.4 1.7 %gather_fusion.2 = f32[8,8,39,128]{3,1,2,0:T(8,128)} fusion(f32[16,8,39,128]{3,1,2,0:T(8,128)S(1)} %all-to-all-done, s32[1024]{0:T(1024)S(1)} %pad_clamp_fusion.1), kind=kCustom, calls=%fused_computation.2 | custom fusion | bytes 2555936 | tf_op jit(solution)/shard_map/gather | solution.py:57
  76.0 1.5 %copy.42 = f32[8,8,39,128]{3,1,0,2:T(8,128)S(1)} copy(f32[8,8,39,128]{3,1,2,0:T(8,128)} %gather_fusion.2) | data formatting | bytes 2555904 | tf_op jit(solution)/shard_map/gather | solution.py:57
  77.5 0.1 pad_maximum_fusion
  77.6 0.3 copy.33
  77.9 61.7 %while.10 = (s32[]{:T(128)}, f32[4,32,128]{2,1,0:T(8,128)S(1)}, s32[]{:T(128)}, s32[4,24]{0,1:T(8,128)S(1)}, f32[72,39,128]{2,1,0:T(8,128)S(1)}, /*index=5*/s32[...) while((s32[]{:T(128)}, f32[4,32,128]{2,1,0:T(8,128)S(1)}, ...), condition=%wide.region_5.6_spmd, body=%wide.region_2.5_spmd.sunk | while | flops 23290952 | bytes 4471535 | solution.py:78
  78.1 0.6 gather_fusion
  78.6 1.0 fusion.33
  80.0 2.7 %multiply_convert_fusion.3 = (bf16[8,128,128]{2,1,0:T(8,128)(2,1)S(1)}, bf16[8,128,128]{2,1,0:T(8,128)(2,1)S(1)}) fusion(f32[8,128,128]{2,1,0:T(8,128)S(1)} %get-tuple-element.169, f32[8,128,128]{2,1,0:T(8,128)S(1)} %get-tuple-element.170, f32[8]{0:T(128)S(1)} %mul.168, f32[8,128]{1,0:T(8,128)S(1)} %broadcast_multiply_fusion.2), kind=kLoop, calls=%fused_computation.13.clone.1 | loop fusion | flops 3145728 | bytes 1576992 | tf_op jit(solution)/shard_map/convert.1
  82.8 0.2 fusion.35
  83.2 0.6 gather_fusion
  83.8 1.0 fusion.33
  85.2 2.7 %multiply_convert_fusion.3 = (bf16[8,128,128]{2,1,0:T(8,128)(2,1)S(1)}, bf16[8,128,128]{2,1,0:T(8,128)(2,1)S(1)}) fusion(f32[8,128,128]{2,1,0:T(8,128)S(1)} %get-tuple-element.169, f32[8,128,128]{2,1,0:T(8,128)S(1)} %get-tuple-element.170, f32[8]{0:T(128)S(1)} %mul.168, f32[8,128]{1,0:T(8,128)S(1)} %broadcast_multiply_fusion.2), kind=kLoop, calls=%fused_computation.13.clone.1 | loop fusion | flops 3145728 | bytes 1576992 | tf_op jit(solution)/shard_map/convert.1
  88.0 0.2 fusion.35
  88.3 0.6 gather_fusion
  88.9 1.0 fusion.33
  90.3 2.7 %multiply_convert_fusion.3 = (bf16[8,128,128]{2,1,0:T(8,128)(2,1)S(1)}, bf16[8,128,128]{2,1,0:T(8,128)(2,1)S(1)}) fusion(f32[8,128,128]{2,1,0:T(8,128)S(1)} %get-tuple-element.169, f32[8,128,128]{2,1,0:T(8,128)S(1)} %get-tuple-element.170, f32[8]{0:T(128)S(1)} %mul.168, f32[8,128]{1,0:T(8,128)S(1)} %broadcast_multiply_fusion.2), kind=kLoop, calls=%fused_computation.13.clone.1 | loop fusion | flops 3145728 | bytes 1576992 | tf_op jit(solution)/shard_map/convert.1
  93.1 0.2 fusion.35
  93.5 0.6 gather_fusion
  94.1 1.0 fusion.33
  95.5 2.7 %multiply_convert_fusion.3 = (bf16[8,128,128]{2,1,0:T(8,128)(2,1)S(1)}, bf16[8,128,128]{2,1,0:T(8,128)(2,1)S(1)}) fusion(f32[8,128,128]{2,1,0:T(8,128)S(1)} %get-tuple-element.169, f32[8,128,128]{2,1,0:T(8,128)S(1)} %get-tuple-element.170, f32[8]{0:T(128)S(1)} %mul.168, f32[8,128]{1,0:T(8,128)S(1)} %broadcast_multiply_fusion.2), kind=kLoop, calls=%fused_computation.13.clone.1 | loop fusion | flops 3145728 | bytes 1576992 | tf_op jit(solution)/shard_map/convert.1
  98.2 0.2 fusion.35
  98.6 0.6 gather_fusion
  99.2 1.0 fusion.33
  100.6 2.7 %multiply_convert_fusion.3 = (bf16[8,128,128]{2,1,0:T(8,128)(2,1)S(1)}, bf16[8,128,128]{2,1,0:T(8,128)(2,1)S(1)}) fusion(f32[8,128,128]{2,1,0:T(8,128)S(1)} %get-tuple-element.169, f32[8,128,128]{2,1,0:T(8,128)S(1)} %get-tuple-element.170, f32[8]{0:T(128)S(1)} %mul.168, f32[8,128]{1,0:T(8,128)S(1)} %broadcast_multiply_fusion.2), kind=kLoop, calls=%fused_computation.13.clone.1 | loop fusion | flops 3145728 | bytes 1576992 | tf_op jit(solution)/shard_map/convert.1
  103.4 0.2 fusion.35
  103.8 0.6 gather_fusion
  104.3 1.0 fusion.33
  105.7 2.7 %multiply_convert_fusion.3 = (bf16[8,128,128]{2,1,0:T(8,128)(2,1)S(1)}, bf16[8,128,128]{2,1,0:T(8,128)(2,1)S(1)}) fusion(f32[8,128,128]{2,1,0:T(8,128)S(1)} %get-tuple-element.169, f32[8,128,128]{2,1,0:T(8,128)S(1)} %get-tuple-element.170, f32[8]{0:T(128)S(1)} %mul.168, f32[8,128]{1,0:T(8,128)S(1)} %broadcast_multiply_fusion.2), kind=kLoop, calls=%fused_computation.13.clone.1 | loop fusion | flops 3145728 | bytes 1576992 | tf_op jit(solution)/shard_map/convert.1
  108.5 0.2 fusion.35
  108.9 0.6 gather_fusion
  109.5 1.0 fusion.33
  110.9 2.7 %multiply_convert_fusion.3 = (bf16[8,128,128]{2,1,0:T(8,128)(2,1)S(1)}, bf16[8,128,128]{2,1,0:T(8,128)(2,1)S(1)}) fusion(f32[8,128,128]{2,1,0:T(8,128)S(1)} %get-tuple-element.169, f32[8,128,128]{2,1,0:T(8,128)S(1)} %get-tuple-element.170, f32[8]{0:T(128)S(1)} %mul.168, f32[8,128]{1,0:T(8,128)S(1)} %broadcast_multiply_fusion.2), kind=kLoop, calls=%fused_computation.13.clone.1 | loop fusion | flops 3145728 | bytes 1576992 | tf_op jit(solution)/shard_map/convert.1
  113.6 0.2 fusion.35
  114.0 0.6 gather_fusion
  114.6 1.0 fusion.33
  116.0 2.7 %multiply_convert_fusion.3 = (bf16[8,128,128]{2,1,0:T(8,128)(2,1)S(1)}, bf16[8,128,128]{2,1,0:T(8,128)(2,1)S(1)}) fusion(f32[8,128,128]{2,1,0:T(8,128)S(1)} %get-tuple-element.169, f32[8,128,128]{2,1,0:T(8,128)S(1)} %get-tuple-element.170, f32[8]{0:T(128)S(1)} %mul.168, f32[8,128]{1,0:T(8,128)S(1)} %broadcast_multiply_fusion.2), kind=kLoop, calls=%fused_computation.13.clone.1 | loop fusion | flops 3145728 | bytes 1576992 | tf_op jit(solution)/shard_map/convert.1
  118.8 0.2 fusion.35
  119.2 0.6 gather_fusion
  119.7 1.0 fusion.33
  121.1 2.7 %multiply_convert_fusion.3 = (bf16[8,128,128]{2,1,0:T(8,128)(2,1)S(1)}, bf16[8,128,128]{2,1,0:T(8,128)(2,1)S(1)}) fusion(f32[8,128,128]{2,1,0:T(8,128)S(1)} %get-tuple-element.169, f32[8,128,128]{2,1,0:T(8,128)S(1)} %get-tuple-element.170, f32[8]{0:T(128)S(1)} %mul.168, f32[8,128]{1,0:T(8,128)S(1)} %broadcast_multiply_fusion.2), kind=kLoop, calls=%fused_computation.13.clone.1 | loop fusion | flops 3145728 | bytes 1576992 | tf_op jit(solution)/shard_map/convert.1
  123.9 0.2 fusion.35
  124.3 0.6 gather_fusion
  124.9 1.0 fusion.33
  126.3 2.7 %multiply_convert_fusion.3 = (bf16[8,128,128]{2,1,0:T(8,128)(2,1)S(1)}, bf16[8,128,128]{2,1,0:T(8,128)(2,1)S(1)}) fusion(f32[8,128,128]{2,1,0:T(8,128)S(1)} %get-tuple-element.169, f32[8,128,128]{2,1,0:T(8,128)S(1)} %get-tuple-element.170, f32[8]{0:T(128)S(1)} %mul.168, f32[8,128]{1,0:T(8,128)S(1)} %broadcast_multiply_fusion.2), kind=kLoop, calls=%fused_computation.13.clone.1 | loop fusion | flops 3145728 | bytes 1576992 | tf_op jit(solution)/shard_map/convert.1
  129.1 0.2 fusion.35
  129.4 0.6 gather_fusion
  130.0 1.0 fusion.33
  131.4 2.7 %multiply_convert_fusion.3 = (bf16[8,128,128]{2,1,0:T(8,128)(2,1)S(1)}, bf16[8,128,128]{2,1,0:T(8,128)(2,1)S(1)}) fusion(f32[8,128,128]{2,1,0:T(8,128)S(1)} %get-tuple-element.169, f32[8,128,128]{2,1,0:T(8,128)S(1)} %get-tuple-element.170, f32[8]{0:T(128)S(1)} %mul.168, f32[8,128]{1,0:T(8,128)S(1)} %broadcast_multiply_fusion.2), kind=kLoop, calls=%fused_computation.13.clone.1 | loop fusion | flops 3145728 | bytes 1576992 | tf_op jit(solution)/shard_map/convert.1
  134.2 0.2 fusion.35
  134.6 0.6 gather_fusion
  135.2 1.0 fusion.33
  136.5 2.7 %multiply_convert_fusion.3 = (bf16[8,128,128]{2,1,0:T(8,128)(2,1)S(1)}, bf16[8,128,128]{2,1,0:T(8,128)(2,1)S(1)}) fusion(f32[8,128,128]{2,1,0:T(8,128)S(1)} %get-tuple-element.169, f32[8,128,128]{2,1,0:T(8,128)S(1)} %get-tuple-element.170, f32[8]{0:T(128)S(1)} %mul.168, f32[8,128]{1,0:T(8,128)S(1)} %broadcast_multiply_fusion.2), kind=kLoop, calls=%fused_computation.13.clone.1 | loop fusion | flops 3145728 | bytes 1576992 | tf_op jit(solution)/shard_map/convert.1
  139.3 0.2 fusion.35
  139.6 0.6 copy_bitcast_fusion.2
  (203 shorter events, 6.6 us)
Async XLA Ops:
  0.0 2.9 %copy-start.2 = (s32[1,8,8]{2,1,0:T(8,128)S(1)}, s32[1,8,8]{2,1,0:T(8,128)}, u32[]{:S(2)}) copy-start(s32[1,8,8]{2,1,0:T(8,128)} %param.16) | copy-start | bytes 772
  3.7 0.7 copy-start.5
  9.1 7.3 %copy-start.1 = (s32[4]{0:T(128)S(1)}, s32[4]{0:T(128)}, u32[]{:S(2)}) copy-start(s32[4]{0:T(128)} %param.18) | copy-start | bytes 52
  9.1 8.6 %copy-start.3 = (s32[4,24]{1,0:T(4,128)S(1)}, s32[4,24]{1,0:T(4,128)}, u32[]{:S(2)}) copy-start(s32[4,24]{1,0:T(4,128)} %param.17) | copy-start | bytes 1156
  9.1 8.7 %copy-start.4 = (s32[4,24]{1,0:T(4,128)S(1)}, s32[4,24]{1,0:T(4,128)}, u32[]{:S(2)}) copy-start(s32[4,24]{1,0:T(4,128)} %param.19) | copy-start | bytes 1156
  9.1 8.8 %copy-start = (f32[3,512]{1,0:T(4,128)S(1)}, f32[3,512]{1,0:T(4,128)}, u32[]{:S(2)}) copy-start(f32[3,512]{1,0:T(4,128)} %param.11) | copy-start | bytes 18436
  9.1 65.3 %all-to-all-start = ((f32[16,8,39,128]{3,1,2,0:T(8,128)}), f32[16,8,39,128]{3,1,2,0:T(8,128)S(1)}, u32[]{:S(2)}, u32[]{:S(2)}) async-start(f32[16,8,39,128]{3,1,2,0:T(8,128)} %scatter_fusion), calls=%async_computation | async-start | bytes 5111808 | tf_op jit(solution)/shard_map/all_to_all | solution.py:56
where the time goes:
time: 141 us; the launch traced here: 140 us
  waiting for transfers between devices  56.5 us (40%)
  other arithmetic  49.6 us (35%)
  local copies, waits for them, and re-layouts  20.4 us (14%)
  starting transfers between devices  7.27 us (5%)
  matrix products  2.4 us (2%)
  blocking collectives  1.92 us (1%)
    all_to_all x1, waiting for transfers between devices, shards(): lax.all_to_all(send_slots, 'dom', split_axis=0, concat_axis=0, tiled=True)  56.5 us
    another operation x24, other arithmetic  32.7 us
    reduce_sum x12, other arithmetic, build_kernel(): normal_part = jnp.sum(offset * source[:, 3:6, :, None], axis=1) * inverse  12.4 us
    all_to_all x1, starting transfers between devices, shards(): lax.all_to_all(send_slots, 'dom', split_axis=0, concat_axis=0, tiled=True)  7.27 us
    gather x12, local copies, waits for them, and re-layouts, add_pair(): source = source_pool[pick_idx]  6.7 us
    gather x2, local copies, waits for them, and re-layouts, shards(): band_tiles = arrived[my_partners]  3.14 us
    scatter x1, local copies, waits for them, and re-layouts, shards(): send_slots = send_slots.at[my_partners].set(part_tiles[band_list[0]])  3.05 us
  transfers between devices with their start and end apart: 1, of which 1 were waited for; matrix products, arithmetic and copies ran while one was open for 1% of the time, Pallas kernels for 0%

commit v1 on v0

--- a/solution.py
+++ b/solution.py
@@ -9,6 +9,18 @@
 coupling = 1.5
 narrow_core = 0.1
 wide_core = 0.4
+
+
+def in_blocks(x, dim, count):
+    shape = x.shape
+    blocks = x.reshape(*shape[:dim], count, shape[dim] // count, *shape[dim + 1 :])
+    return jnp.moveaxis(blocks, dim, 0)
+
+
+def laid_out(pieces, dim):
+    pieces = jnp.moveaxis(pieces, 0, dim)
+    shape = pieces.shape
+    return pieces.reshape(*shape[:dim], shape[dim] * shape[dim + 1], *shape[dim + 2 :])
 
 
 def build_kernel(target_pos, source, valid_mask, flag_row):
@@ -53,7 +65,14 @@
     my_partners = partners[0]
     send_slots = jnp.zeros((n_dom, band_size, channels, TILE), jnp.float32)
     send_slots = send_slots.at[my_partners].set(part_tiles[band_list[0]])
-    arrived = lax.all_to_all(send_slots, "dom", split_axis=0, concat_axis=0, tiled=True)
+    length, index = (lax.axis_size("dom"), lax.axis_index("dom"))
+    blocks = in_blocks(send_slots, 0, length)
+    outs = [blocks[index]]
+    for step in range(1, length):
+        sent = blocks[(index + step) % length]
+        outs.append(lax.ppermute(sent, "dom", [(i, (i + step) % length) for i in range(length)]))
+    blocks = jnp.stack(outs)[(index - jnp.arange(length)) % length]
+    arrived = laid_out(blocks, 0)
     band_tiles = arrived[my_partners]
     source_pool = jnp.concatenate([part_tiles, band_tiles.reshape(-1, channels, TILE)], axis=0)
     target_pos = positions.reshape(3, local_tiles, TILE).transpose(1, 0, 2)

time: 141 us -> 151 us (1.071)
  starting transfers between devices: 7.27 us -> 54.1 us
  waiting for transfers between devices: 56.5 us -> 11.3 us
  local copies, waits for them, and re-layouts: 20.4 us -> 26.3 us
  other arithmetic: 49.6 us -> 52.2 us
    all_to_all x1 -> x0, waiting for transfers between devices: 56.5 us -> none  [shards(): lax.all_to_all(send_slots, 'dom', split_axis=0, concat_axis=0, tiled=True)]
    ppermute x0 -> x15, starting transfers between devices: none -> 54.1 us  [shards(): lax.ppermute(sent, 'dom', [(i, (i + step) % length) for i in range(length)])]
    ppermute x0 -> x15, waiting for transfers between devices: none -> 11.3 us  [shards(): lax.ppermute(sent, 'dom', [(i, (i + step) % length) for i in range(length)])]
    all_to_all x1 -> x0, starting transfers between devices: 7.27 us -> none  [shards(): lax.all_to_all(send_slots, 'dom', split_axis=0, concat_axis=0, tiled=True)]
    gather x0 -> x1, local copies, waits for them, and re-layouts: none -> 2.55 us  [shards(): blocks = jnp.stack(outs)[(index - jnp.arange(length)) % length]]
    unnamed x13 -> x32, local copies, waits for them, and re-layouts: 0.46 us -> 2.86 us
  transfers between devices with their start and end apart: 1 -> 15, of which waited for: 1 -> 5; matrix products, arithmetic and copies ran while one was open for 1% -> 2% of each run, Pallas kernels for 0% -> 0%
where the time goes in v1:
time: 151 us; the launch traced here: 150 us
  starting transfers between devices  54.1 us (36%)
  other arithmetic  52.2 us (35%)
  local copies, waits for them, and re-layouts  26.3 us (17%)
  waiting for transfers between devices  11.3 us (7%)
  matrix products  2.37 us (2%)
  blocking collectives  1.92 us (1%)
    ppermute x15, starting transfers between devices, shards(): lax.ppermute(sent, 'dom', [(i, (i + step) % length) for i in range(length)])  54.1 us
    another operation x24, other arithmetic  32.7 us
    reduce_sum x12, other arithmetic, build_kernel(): normal_part = jnp.sum(offset * source[:, 3:6, :, None], axis=1) * inverse  12.4 us
    ppermute x15, waiting for transfers between devices, shards(): lax.ppermute(sent, 'dom', [(i, (i + step) % length) for i in range(length)])  11.3 us
    gather x12, local copies, waits for them, and re-layouts, add_pair(): source = source_pool[pick_idx]  6.7 us
    gather x2, local copies, waits for them, and re-layouts, shards(): band_tiles = arrived[my_partners]  3.29 us
  transfers between devices with their start and end apart: 15, of which 5 were waited for; matrix products, arithmetic and copies ran while one was open for 2% of the time, Pallas kernels for 0%

profile of v1, /device:TPU:16, one launch (start us, length us, event | category | flops | bytes accessed | tf_op | source)
XLA Modules:
  0.0 150.4 jit_solution(10772825123293682779)
XLA Ops:
  0.0 0.7 fusion.20
  0.7 0.7 compare_select_fusion.2
  1.4 0.9 pad_maximum_fusion.1
  2.3 1.9 %all_gather.3 = f32[39,1024]{1,0:T(8,128)S(1)} all-gather(f32[39,512]{1,0:T(8,128)S(1)} %pad_maximum_fusion.1), channel_id=1, replica_groups=mesh['dom'=16,'tgt'=2] {'tgt'}, dimensions={1}, use_global_device_ids=true | all-gather | bytes 239616 | tf_op jit(solution)/shard_map/all_gather | solution.py:61
  4.3 0.6 pad_clamp_fusion.1
  4.9 0.7 gather_fusion.1
  5.6 1.3 copy.29
  7.1 2.1 %scatter_fusion = f32[16,8,39,128]{3,1,2,0:T(8,128)S(1)} fusion(f32[16,8,39,128]{3,1,2,0:T(8,128)S(1)} %broadcast_in_dim.16, s32[8]{0:T(128)S(1)} %fusion.20, f32[8,8,39,128]{3,1,2,0:T(8,128)} %copy.29), kind=kCustom, calls=%fused_computation.4 | custom fusion | bytes 3833888 | tf_op jit(solution)/shard_map/scatter | solution.py:67
  9.2 1.4 constant_dynamic-slice_fusion
  10.7 1.5 collective-permute-start
  12.2 1.5 %collective-permute-start.1 = (f32[1,8,39,128]{3,1,2,0:T(8,128)}, f32[1,8,39,128]{3,1,2,0:T(8,128)S(1)}, u32[]{:S(2)}, u32[]{:S(2)}) collective-permute-start(f32[1,8,39,128]{3,1,2,0:T(8,128)} %get-tuple-element.119), channel_id=1, source_target_pairs={{0,4},{2,6},{4,8},{6,10},{8,12},{10,14},{12,16},{14,18},{16,20},{1... | collective-permute-start | bytes 479240 | tf_op jit(solution)/shard_map/ppermute | solution.py:73
  13.7 2.4 %collective-permute-start.2 = (f32[1,8,39,128]{3,1,2,0:T(8,128)}, f32[1,8,39,128]{3,1,2,0:T(8,128)S(1)}, u32[]{:S(2)}, u32[]{:S(2)}) collective-permute-start(f32[1,8,39,128]{3,1,2,0:T(8,128)} %get-tuple-element.118), channel_id=1, source_target_pairs={{0,6},{2,8},{4,10},{6,12},{8,14},{10,16},{12,18},{14,20},{16,22},{... | collective-permute-start | bytes 479240 | tf_op jit(solution)/shard_map/ppermute | solution.py:73
  16.3 1.6 %collective-permute-start.4 = (f32[1,8,39,128]{3,1,2,0:T(8,128)}, f32[1,8,39,128]{3,1,2,0:T(8,128)S(1)}, u32[]{:S(2)}, u32[]{:S(2)}) collective-permute-start(f32[1,8,39,128]{3,1,2,0:T(8,128)} %get-tuple-element.116), channel_id=1, source_target_pairs={{0,10},{2,12},{4,14},{6,16},{8,18},{10,20},{12,22},{14,24},{16,26}... | collective-permute-start | bytes 479240 | tf_op jit(solution)/shard_map/ppermute | solution.py:73
  18.0 0.6 pad_clamp_fusion.2
  18.6 0.6 reduce_max.9
  19.9 0.8 copy.34
  20.7 0.9 collective-permute-done
  21.6 2.1 %collective-permute-start.5 = (f32[1,8,39,128]{3,1,2,0:T(8,128)}, f32[1,8,39,128]{3,1,2,0:T(8,128)S(1)}, u32[]{:S(2)}, u32[]{:S(2)}) collective-permute-start(f32[1,8,39,128]{3,1,2,0:T(8,128)} %get-tuple-element.115), channel_id=1, source_target_pairs={{0,12},{2,14},{4,16},{6,18},{8,20},{10,22},{12,24},{14,26},{16,28}... | collective-permute-start | bytes 479240 | tf_op jit(solution)/shard_map/ppermute | solution.py:73
  23.7 0.9 bitcast_dynamic-update-slice_fusion.14
  24.7 1.7 %collective-permute-start.6 = (f32[1,8,39,128]{3,1,2,0:T(8,128)}, f32[1,8,39,128]{3,1,2,0:T(8,128)S(1)}, u32[]{:S(2)}, u32[]{:S(2)}) collective-permute-start(f32[1,8,39,128]{3,1,2,0:T(8,128)} %get-tuple-element.114), channel_id=1, source_target_pairs={{0,14},{2,16},{4,18},{6,20},{8,22},{10,24},{12,26},{14,28},{16,30}... | collective-permute-start | bytes 479240 | tf_op jit(solution)/shard_map/ppermute | solution.py:73
  26.4 2.7 %collective-permute-start.7 = (f32[1,8,39,128]{3,1,2,0:T(8,128)}, f32[1,8,39,128]{3,1,2,0:T(8,128)S(1)}, u32[]{:S(2)}, u32[]{:S(2)}) collective-permute-start(f32[1,8,39,128]{3,1,2,0:T(8,128)} %get-tuple-element.113), channel_id=1, source_target_pairs={{0,16},{2,18},{4,20},{6,22},{8,24},{10,26},{12,28},{14,30},{16,0},... | collective-permute-start | bytes 479240 | tf_op jit(solution)/shard_map/ppermute | solution.py:73
  29.3 5.6 %collective-permute-done.4 = f32[1,8,39,128]{3,1,2,0:T(8,128)S(1)} collective-permute-done((f32[1,8,39,128]{3,1,2,0:T(8,128)}, f32[1,8,39,128]{3,1,2,0:T(8,128)S(1)}, u32[]{:S(2)}, u32[]{:S(2)}) %collective-permute-start.4) | collective-permute-done | bytes 159776 | tf_op jit(solution)/shard_map/ppermute | solution.py:73
  34.9 22.7 %collective-permute-start.9 = (f32[1,8,39,128]{3,1,2,0:T(8,128)}, f32[1,8,39,128]{3,1,2,0:T(8,128)S(1)}, u32[]{:S(2)}, u32[]{:S(2)}) collective-permute-start(f32[1,8,39,128]{3,1,2,0:T(8,128)} %get-tuple-element.111), channel_id=1, source_target_pairs={{0,20},{2,22},{4,24},{6,26},{8,28},{10,30},{12,0},{14,2},{16,4},{1... | collective-permute-start | bytes 479240 | tf_op jit(solution)/shard_map/ppermute | solution.py:73
  57.8 5.7 %collective-permute-start.12 = (f32[1,8,39,128]{3,1,2,0:T(8,128)S(1)}, f32[1,8,39,128]{3,1,2,0:T(8,128)S(1)}, u32[]{:S(2)}, u32[]{:S(2)}) collective-permute-start(f32[1,8,39,128]{3,1,2,0:T(8,128)S(1)} %copy-done.3), channel_id=1, source_target_pairs={{0,26},{2,28},{4,30},{6,0},{8,2},{10,4},{12,6},{14,8},{16,10},{18,... | collective-permute-start | bytes 479240 | tf_op jit(solution)/shard_map/ppermute | solution.py:73
  63.5 6.8 %collective-permute-start.13 = (f32[1,8,39,128]{3,1,2,0:T(8,128)S(1)}, f32[1,8,39,128]{3,1,2,0:T(8,128)S(1)}, u32[]{:S(2)}, u32[]{:S(2)}) collective-permute-start(f32[1,8,39,128]{3,1,2,0:T(8,128)S(1)} %copy-done.2), channel_id=1, source_target_pairs={{0,28},{2,30},{4,0},{6,2},{8,4},{10,6},{12,8},{14,10},{16,12},{18,... | collective-permute-start | bytes 479240 | tf_op jit(solution)/shard_map/ppermute | solution.py:73
  70.4 4.8 %collective-permute-start.14 = (f32[1,8,39,128]{3,1,2,0:T(8,128)S(1)}, f32[1,8,39,128]{3,1,2,0:T(8,128)S(1)}, u32[]{:S(2)}, u32[]{:S(2)}) collective-permute-start(f32[1,8,39,128]{3,1,2,0:T(8,128)S(1)} %copy-done.1), channel_id=1, source_target_pairs={{0,30},{2,0},{4,2},{6,4},{8,6},{10,8},{12,10},{14,12},{16,14},{18,... | collective-permute-start | bytes 479240 | tf_op jit(solution)/shard_map/ppermute | solution.py:73
  75.3 1.4 collective-permute-done.12
  76.8 1.7 %collective-permute-done.13 = f32[1,8,39,128]{3,1,2,0:T(8,128)S(1)} collective-permute-done((f32[1,8,39,128]{3,1,2,0:T(8,128)S(1)}, f32[1,8,39,128]{3,1,2,0:T(8,128)S(1)}, u32[]{:S(2)}, u32[]{:S(2)}) %collective-permute-start.13) | collective-permute-done | bytes 159776 | tf_op jit(solution)/shard_map/ppermute | solution.py:73
  78.5 1.7 %collective-permute-done.14 = f32[1,8,39,128]{3,1,2,0:T(8,128)S(1)} collective-permute-done((f32[1,8,39,128]{3,1,2,0:T(8,128)S(1)}, f32[1,8,39,128]{3,1,2,0:T(8,128)S(1)}, u32[]{:S(2)}, u32[]{:S(2)}) %collective-permute-start.14) | collective-permute-done | bytes 159776 | tf_op jit(solution)/shard_map/ppermute | solution.py:73
  80.2 1.5 copy-done
  81.7 2.6 %gather_fusion.2 = f32[16,8,39,128]{3,1,2,0:T(8,128)S(1)} fusion(f32[16,8,39,128]{3,1,2,0:T(8,128)} %bitcast.83, s32[1024]{0:T(1024)} %pad_clamp_fusion.2), kind=kCustom, calls=%fused_computation.2 | custom fusion | bytes 5111872 | tf_op jit(solution)/shard_map/gather | solution.py:74
  84.2 1.8 %gather_fusion.3 = f32[8,8,39,128]{3,1,2,0:T(8,128)} fusion(f32[16,8,39,128]{3,1,2,0:T(8,128)S(1)} %gather_fusion.2, s32[1024]{0:T(1024)} %get-tuple-element.123), kind=kCustom, calls=%fused_computation.3 | custom fusion | bytes 2555936 | tf_op jit(solution)/shard_map/gather | solution.py:76
  86.1 1.5 copy.42
  88.2 61.6 %while.10 = (s32[]{:T(128)}, f32[4,32,128]{2,1,0:T(8,128)S(1)}, s32[]{:T(128)}, s32[4,24]{0,1:T(8,128)S(1)}, f32[72,39,128]{2,1,0:T(8,128)S(1)}, /*index=5*/s32[...) while((s32[]{:T(128)}, f32[4,32,128]{2,1,0:T(8,128)S(1)}, ...), condition=%wide.region_5.6_spmd, body=%wide.region_2.5_spmd.sunk | while | flops 23290952 | bytes 4471535 | solution.py:97
  88.9 1.0 fusion.35
  90.3 2.7 %multiply_convert_fusion.3 = (bf16[8,128,128]{2,1,0:T(8,128)(2,1)S(1)}, bf16[8,128,128]{2,1,0:T(8,128)(2,1)S(1)}) fusion(f32[8,128,128]{2,1,0:T(8,128)S(1)} %get-tuple-element.186, f32[8,128,128]{2,1,0:T(8,128)S(1)} %get-tuple-element.187, f32[8]{0:T(128)S(1)} %mul.168, f32[8,128]{1,0:T(8,128)S(1)} %broadcast_multiply_fusion.2), kind=kLoop, calls=%fused_computation.14.clone.1 | loop fusion | flops 3145728 | bytes 1576992 | tf_op jit(solution)/shard_map/convert.1
  93.4 0.6 gather_fusion
  94.0 1.0 fusion.35
  95.4 2.7 %multiply_convert_fusion.3 = (bf16[8,128,128]{2,1,0:T(8,128)(2,1)S(1)}, bf16[8,128,128]{2,1,0:T(8,128)(2,1)S(1)}) fusion(f32[8,128,128]{2,1,0:T(8,128)S(1)} %get-tuple-element.186, f32[8,128,128]{2,1,0:T(8,128)S(1)} %get-tuple-element.187, f32[8]{0:T(128)S(1)} %mul.168, f32[8,128]{1,0:T(8,128)S(1)} %broadcast_multiply_fusion.2), kind=kLoop, calls=%fused_computation.14.clone.1 | loop fusion | flops 3145728 | bytes 1576992 | tf_op jit(solution)/shard_map/convert.1
  99.2 1.0 fusion.35
  100.5 2.7 %multiply_convert_fusion.3 = (bf16[8,128,128]{2,1,0:T(8,128)(2,1)S(1)}, bf16[8,128,128]{2,1,0:T(8,128)(2,1)S(1)}) fusion(f32[8,128,128]{2,1,0:T(8,128)S(1)} %get-tuple-element.186, f32[8,128,128]{2,1,0:T(8,128)S(1)} %get-tuple-element.187, f32[8]{0:T(128)S(1)} %mul.168, f32[8,128]{1,0:T(8,128)S(1)} %broadcast_multiply_fusion.2), kind=kLoop, calls=%fused_computation.14.clone.1 | loop fusion | flops 3145728 | bytes 1576992 | tf_op jit(solution)/shard_map/convert.1
  104.3 1.0 fusion.35
  105.7 2.7 %multiply_convert_fusion.3 = (bf16[8,128,128]{2,1,0:T(8,128)(2,1)S(1)}, bf16[8,128,128]{2,1,0:T(8,128)(2,1)S(1)}) fusion(f32[8,128,128]{2,1,0:T(8,128)S(1)} %get-tuple-element.186, f32[8,128,128]{2,1,0:T(8,128)S(1)} %get-tuple-element.187, f32[8]{0:T(128)S(1)} %mul.168, f32[8,128]{1,0:T(8,128)S(1)} %broadcast_multiply_fusion.2), kind=kLoop, calls=%fused_computation.14.clone.1 | loop fusion | flops 3145728 | bytes 1576992 | tf_op jit(solution)/shard_map/convert.1
  109.4 1.0 fusion.35
  110.8 2.7 %multiply_convert_fusion.3 = (bf16[8,128,128]{2,1,0:T(8,128)(2,1)S(1)}, bf16[8,128,128]{2,1,0:T(8,128)(2,1)S(1)}) fusion(f32[8,128,128]{2,1,0:T(8,128)S(1)} %get-tuple-element.186, f32[8,128,128]{2,1,0:T(8,128)S(1)} %get-tuple-element.187, f32[8]{0:T(128)S(1)} %mul.168, f32[8,128]{1,0:T(8,128)S(1)} %broadcast_multiply_fusion.2), kind=kLoop, calls=%fused_computation.14.clone.1 | loop fusion | flops 3145728 | bytes 1576992 | tf_op jit(solution)/shard_map/convert.1
  114.0 0.6 gather_fusion
  114.6 1.0 fusion.35
  116.0 2.7 %multiply_convert_fusion.3 = (bf16[8,128,128]{2,1,0:T(8,128)(2,1)S(1)}, bf16[8,128,128]{2,1,0:T(8,128)(2,1)S(1)}) fusion(f32[8,128,128]{2,1,0:T(8,128)S(1)} %get-tuple-element.186, f32[8,128,128]{2,1,0:T(8,128)S(1)} %get-tuple-element.187, f32[8]{0:T(128)S(1)} %mul.168, f32[8,128]{1,0:T(8,128)S(1)} %broadcast_multiply_fusion.2), kind=kLoop, calls=%fused_computation.14.clone.1 | loop fusion | flops 3145728 | bytes 1576992 | tf_op jit(solution)/shard_map/convert.1
  119.7 1.0 fusion.35
  121.1 2.7 %multiply_convert_fusion.3 = (bf16[8,128,128]{2,1,0:T(8,128)(2,1)S(1)}, bf16[8,128,128]{2,1,0:T(8,128)(2,1)S(1)}) fusion(f32[8,128,128]{2,1,0:T(8,128)S(1)} %get-tuple-element.186, f32[8,128,128]{2,1,0:T(8,128)S(1)} %get-tuple-element.187, f32[8]{0:T(128)S(1)} %mul.168, f32[8,128]{1,0:T(8,128)S(1)} %broadcast_multiply_fusion.2), kind=kLoop, calls=%fused_computation.14.clone.1 | loop fusion | flops 3145728 | bytes 1576992 | tf_op jit(solution)/shard_map/convert.1
  124.3 0.6 gather_fusion
  124.8 1.0 fusion.35
  126.2 2.7 %multiply_convert_fusion.3 = (bf16[8,128,128]{2,1,0:T(8,128)(2,1)S(1)}, bf16[8,128,128]{2,1,0:T(8,128)(2,1)S(1)}) fusion(f32[8,128,128]{2,1,0:T(8,128)S(1)} %get-tuple-element.186, f32[8,128,128]{2,1,0:T(8,128)S(1)} %get-tuple-element.187, f32[8]{0:T(128)S(1)} %mul.168, f32[8,128]{1,0:T(8,128)S(1)} %broadcast_multiply_fusion.2), kind=kLoop, calls=%fused_computation.14.clone.1 | loop fusion | flops 3145728 | bytes 1576992 | tf_op jit(solution)/shard_map/convert.1
  130.0 1.0 fusion.35
  131.4 2.7 %multiply_convert_fusion.3 = (bf16[8,128,128]{2,1,0:T(8,128)(2,1)S(1)}, bf16[8,128,128]{2,1,0:T(8,128)(2,1)S(1)}) fusion(f32[8,128,128]{2,1,0:T(8,128)S(1)} %get-tuple-element.186, f32[8,128,128]{2,1,0:T(8,128)S(1)} %get-tuple-element.187, f32[8]{0:T(128)S(1)} %mul.168, f32[8,128]{1,0:T(8,128)S(1)} %broadcast_multiply_fusion.2), kind=kLoop, calls=%fused_computation.14.clone.1 | loop fusion | flops 3145728 | bytes 1576992 | tf_op jit(solution)/shard_map/convert.1
  134.5 0.6 gather_fusion
  135.1 1.0 fusion.35
  136.5 2.7 %multiply_convert_fusion.3 = (bf16[8,128,128]{2,1,0:T(8,128)(2,1)S(1)}, bf16[8,128,128]{2,1,0:T(8,128)(2,1)S(1)}) fusion(f32[8,128,128]{2,1,0:T(8,128)S(1)} %get-tuple-element.186, f32[8,128,128]{2,1,0:T(8,128)S(1)} %get-tuple-element.187, f32[8]{0:T(128)S(1)} %mul.168, f32[8,128]{1,0:T(8,128)S(1)} %broadcast_multiply_fusion.2), kind=kLoop, calls=%fused_computation.14.clone.1 | loop fusion | flops 3145728 | bytes 1576992 | tf_op jit(solution)/shard_map/convert.1
  139.7 0.6 gather_fusion
  140.2 1.0 fusion.35
  141.6 2.7 %multiply_convert_fusion.3 = (bf16[8,128,128]{2,1,0:T(8,128)(2,1)S(1)}, bf16[8,128,128]{2,1,0:T(8,128)(2,1)S(1)}) fusion(f32[8,128,128]{2,1,0:T(8,128)S(1)} %get-tuple-element.186, f32[8,128,128]{2,1,0:T(8,128)S(1)} %get-tuple-element.187, f32[8]{0:T(128)S(1)} %mul.168, f32[8,128]{1,0:T(8,128)S(1)} %broadcast_multiply_fusion.2), kind=kLoop, calls=%fused_computation.14.clone.1 | loop fusion | flops 3145728 | bytes 1576992 | tf_op jit(solution)/shard_map/convert.1
  145.4 1.0 fusion.35
  146.8 2.7 %multiply_convert_fusion.3 = (bf16[8,128,128]{2,1,0:T(8,128)(2,1)S(1)}, bf16[8,128,128]{2,1,0:T(8,128)(2,1)S(1)}) fusion(f32[8,128,128]{2,1,0:T(8,128)S(1)} %get-tuple-element.186, f32[8,128,128]{2,1,0:T(8,128)S(1)} %get-tuple-element.187, f32[8]{0:T(128)S(1)} %mul.168, f32[8,128]{1,0:T(8,128)S(1)} %broadcast_multiply_fusion.2), kind=kLoop, calls=%fused_computation.14.clone.1 | loop fusion | flops 3145728 | bytes 1576992 | tf_op jit(solution)/shard_map/convert.1
  149.8 0.6 copy_bitcast_fusion.2
  (254 shorter events, 14.3 us)
Async XLA Ops:
  9.2 8.8 %copy-start.4 = (f32[3,512]{1,0:T(4,128)S(1)}, f32[3,512]{1,0:T(4,128)}, u32[]{:S(2)}) copy-start(f32[3,512]{1,0:T(4,128)} %param.11) | copy-start | bytes 18436
  9.2 9.4 %copy-start.5 = (s32[4]{0:T(128)S(1)}, s32[4]{0:T(128)}, u32[]{:S(2)}) copy-start(s32[4]{0:T(128)} %param.18) | copy-start | bytes 52
  9.2 10.6 %copy-start.7 = (s32[4,24]{1,0:T(4,128)S(1)}, s32[4,24]{1,0:T(4,128)}, u32[]{:S(2)}) copy-start(s32[4,24]{1,0:T(4,128)} %param.17) | copy-start | bytes 1156
  10.7 11.0 %collective-permute-start = (f32[1,8,39,128]{3,1,2,0:T(8,128)}, f32[1,8,39,128]{3,1,2,0:T(8,128)}, u32[]{:S(2)}, u32[]{:S(2)}) collective-permute-start(f32[1,8,39,128]{3,1,2,0:T(8,128)} %get-tuple-element.120), channel_id=1, source_target_pairs={{0,2},{2,4},{4,6},{6,8},{8,10},{10,12},{12,14},{14,16},{16,18},{18... | collective-permute-start | bytes 479240 | tf_op jit(solution)/shard_map/ppermute | solution.py:73
  12.2 12.5 %collective-permute-start.1 = (f32[1,8,39,128]{3,1,2,0:T(8,128)}, f32[1,8,39,128]{3,1,2,0:T(8,128)S(1)}, u32[]{:S(2)}, u32[]{:S(2)}) collective-permute-start(f32[1,8,39,128]{3,1,2,0:T(8,128)} %get-tuple-element.119), channel_id=1, source_target_pairs={{0,4},{2,6},{4,8},{6,10},{8,12},{10,14},{12,16},{14,18},{16,20},{1... | collective-permute-start | bytes 479240 | tf_op jit(solution)/shard_map/ppermute | solution.py:73
  13.7 12.7 %collective-permute-start.2 = (f32[1,8,39,128]{3,1,2,0:T(8,128)}, f32[1,8,39,128]{3,1,2,0:T(8,128)S(1)}, u32[]{:S(2)}, u32[]{:S(2)}) collective-permute-start(f32[1,8,39,128]{3,1,2,0:T(8,128)} %get-tuple-element.118), channel_id=1, source_target_pairs={{0,6},{2,8},{4,10},{6,12},{8,14},{10,16},{12,18},{14,20},{16,22},{... | collective-permute-start | bytes 479240 | tf_op jit(solution)/shard_map/ppermute | solution.py:73
  16.1 13.0 %collective-permute-start.3 = (f32[1,8,39,128]{3,1,2,0:T(8,128)}, f32[1,8,39,128]{3,1,2,0:T(8,128)S(1)}, u32[]{:S(2)}, u32[]{:S(2)}) collective-permute-start(f32[1,8,39,128]{3,1,2,0:T(8,128)} %get-tuple-element.117), channel_id=1, source_target_pairs={{0,8},{2,10},{4,12},{6,14},{8,16},{10,18},{12,20},{14,22},{16,24},... | collective-permute-start | bytes 479240 | tf_op jit(solution)/shard_map/ppermute | solution.py:73
  16.3 18.5 %collective-permute-start.4 = (f32[1,8,39,128]{3,1,2,0:T(8,128)}, f32[1,8,39,128]{3,1,2,0:T(8,128)S(1)}, u32[]{:S(2)}, u32[]{:S(2)}) collective-permute-start(f32[1,8,39,128]{3,1,2,0:T(8,128)} %get-tuple-element.116), channel_id=1, source_target_pairs={{0,10},{2,12},{4,14},{6,16},{8,18},{10,20},{12,22},{14,24},{16,26}... | collective-permute-start | bytes 479240 | tf_op jit(solution)/shard_map/ppermute | solution.py:73
  20.7 37.1 %copy-start.3 = (f32[1,8,39,128]{3,1,2,0:T(8,128)S(1)}, f32[1,8,39,128]{3,1,2,0:T(8,128)}, u32[]{:S(2)}) copy-start(f32[1,8,39,128]{3,1,2,0:T(8,128)} %get-tuple-element.108) | copy-start | bytes 479236
  20.7 42.8 %copy-start.2 = (f32[1,8,39,128]{3,1,2,0:T(8,128)S(1)}, f32[1,8,39,128]{3,1,2,0:T(8,128)}, u32[]{:S(2)}) copy-start(f32[1,8,39,128]{3,1,2,0:T(8,128)} %get-tuple-element.107) | copy-start | bytes 479236
  20.7 49.7 %copy-start.1 = (f32[1,8,39,128]{3,1,2,0:T(8,128)S(1)}, f32[1,8,39,128]{3,1,2,0:T(8,128)}, u32[]{:S(2)}) copy-start(f32[1,8,39,128]{3,1,2,0:T(8,128)} %get-tuple-element.106) | copy-start | bytes 479236
  21.6 35.9 %collective-permute-start.5 = (f32[1,8,39,128]{3,1,2,0:T(8,128)}, f32[1,8,39,128]{3,1,2,0:T(8,128)S(1)}, u32[]{:S(2)}, u32[]{:S(2)}) collective-permute-start(f32[1,8,39,128]{3,1,2,0:T(8,128)} %get-tuple-element.115), channel_id=1, source_target_pairs={{0,12},{2,14},{4,16},{6,18},{8,20},{10,22},{12,24},{14,26},{16,28}... | collective-permute-start | bytes 479240 | tf_op jit(solution)/shard_map/ppermute | solution.py:73
  24.7 33.0 %collective-permute-start.6 = (f32[1,8,39,128]{3,1,2,0:T(8,128)}, f32[1,8,39,128]{3,1,2,0:T(8,128)S(1)}, u32[]{:S(2)}, u32[]{:S(2)}) collective-permute-start(f32[1,8,39,128]{3,1,2,0:T(8,128)} %get-tuple-element.114), channel_id=1, source_target_pairs={{0,14},{2,16},{4,18},{6,20},{8,22},{10,24},{12,26},{14,28},{16,30}... | collective-permute-start | bytes 479240 | tf_op jit(solution)/shard_map/ppermute | solution.py:73
  26.4 31.3 %collective-permute-start.7 = (f32[1,8,39,128]{3,1,2,0:T(8,128)}, f32[1,8,39,128]{3,1,2,0:T(8,128)S(1)}, u32[]{:S(2)}, u32[]{:S(2)}) collective-permute-start(f32[1,8,39,128]{3,1,2,0:T(8,128)} %get-tuple-element.113), channel_id=1, source_target_pairs={{0,16},{2,18},{4,20},{6,22},{8,24},{10,26},{12,28},{14,30},{16,0},... | collective-permute-start | bytes 479240 | tf_op jit(solution)/shard_map/ppermute | solution.py:73
  29.1 34.4 %collective-permute-start.8 = (f32[1,8,39,128]{3,1,2,0:T(8,128)}, f32[1,8,39,128]{3,1,2,0:T(8,128)S(1)}, u32[]{:S(2)}, u32[]{:S(2)}) collective-permute-start(f32[1,8,39,128]{3,1,2,0:T(8,128)} %get-tuple-element.112), channel_id=1, source_target_pairs={{0,18},{2,20},{4,22},{6,24},{8,26},{10,28},{12,30},{14,0},{16,2},{... | collective-permute-start | bytes 479240 | tf_op jit(solution)/shard_map/ppermute | solution.py:73
  34.9 35.5 %collective-permute-start.9 = (f32[1,8,39,128]{3,1,2,0:T(8,128)}, f32[1,8,39,128]{3,1,2,0:T(8,128)S(1)}, u32[]{:S(2)}, u32[]{:S(2)}) collective-permute-start(f32[1,8,39,128]{3,1,2,0:T(8,128)} %get-tuple-element.111), channel_id=1, source_target_pairs={{0,20},{2,22},{4,24},{6,26},{8,28},{10,30},{12,0},{14,2},{16,4},{1... | collective-permute-start | bytes 479240 | tf_op jit(solution)/shard_map/ppermute | solution.py:73
  57.6 17.7 %collective-permute-start.10 = (f32[1,8,39,128]{3,1,2,0:T(8,128)}, f32[1,8,39,128]{3,1,2,0:T(8,128)S(1)}, u32[]{:S(2)}, u32[]{:S(2)}) collective-permute-start(f32[1,8,39,128]{3,1,2,0:T(8,128)} %get-tuple-element.110), channel_id=1, source_target_pairs={{0,22},{2,24},{4,26},{6,28},{8,30},{10,0},{12,2},{14,4},{16,6},{18... | collective-permute-start | bytes 479240 | tf_op jit(solution)/shard_map/ppermute | solution.py:73
  57.7 17.6 %collective-permute-start.11 = (f32[1,8,39,128]{3,1,2,0:T(8,128)S(1)}, f32[1,8,39,128]{3,1,2,0:T(8,128)S(1)}, u32[]{:S(2)}, u32[]{:S(2)}) collective-permute-start(f32[1,8,39,128]{3,1,2,0:T(8,128)S(1)} %get-tuple-element.109), channel_id=1, source_target_pairs={{0,24},{2,26},{4,28},{6,30},{8,0},{10,2},{12,4},{14,6},{16,8},{18,... | collective-permute-start | bytes 479240 | tf_op jit(solution)/shard_map/ppermute | solution.py:73
  57.8 19.0 %collective-permute-start.12 = (f32[1,8,39,128]{3,1,2,0:T(8,128)S(1)}, f32[1,8,39,128]{3,1,2,0:T(8,128)S(1)}, u32[]{:S(2)}, u32[]{:S(2)}) collective-permute-start(f32[1,8,39,128]{3,1,2,0:T(8,128)S(1)} %copy-done.3), channel_id=1, source_target_pairs={{0,26},{2,28},{4,30},{6,0},{8,2},{10,4},{12,6},{14,8},{16,10},{18,... | collective-permute-start | bytes 479240 | tf_op jit(solution)/shard_map/ppermute | solution.py:73
  63.5 14.9 %collective-permute-start.13 = (f32[1,8,39,128]{3,1,2,0:T(8,128)S(1)}, f32[1,8,39,128]{3,1,2,0:T(8,128)S(1)}, u32[]{:S(2)}, u32[]{:S(2)}) collective-permute-start(f32[1,8,39,128]{3,1,2,0:T(8,128)S(1)} %copy-done.2), channel_id=1, source_target_pairs={{0,28},{2,30},{4,0},{6,2},{8,4},{10,6},{12,8},{14,10},{16,12},{18,... | collective-permute-start | bytes 479240 | tf_op jit(solution)/shard_map/ppermute | solution.py:73
  70.4 9.8 %collective-permute-start.14 = (f32[1,8,39,128]{3,1,2,0:T(8,128)S(1)}, f32[1,8,39,128]{3,1,2,0:T(8,128)S(1)}, u32[]{:S(2)}, u32[]{:S(2)}) collective-permute-start(f32[1,8,39,128]{3,1,2,0:T(8,128)S(1)} %copy-done.1), channel_id=1, source_target_pairs={{0,30},{2,0},{4,2},{6,4},{8,6},{10,8},{12,10},{14,12},{16,14},{18,... | collective-permute-start | bytes 479240 | tf_op jit(solution)/shard_map/ppermute | solution.py:73
  80.2 1.5 copy-start
  87.5 0.7 copy-start.6
